TPU v7x, 256 devices: a whole 4x4x8 slice. The times are simulated.
256 devices in a mesh: elem: 8 (over z), tm: 32 (over y, x, core).
Axes of the slice: x: 4, y: 4, z: 8, core: 2. Of those that a mesh axis runs over, the one named last changes fastest.
Arguments:
- samples: bfloat16 [24576, 2048], P('tm', 'elem'), may hold values from -160 to 160
- taps_weight: bfloat16 [16, 2048, 512], P(None, 'elem'), may hold values from -0.046875 to 0.046875
- retain: float32 [24576], P('tm')
Outputs:
- whitened: float32 [512, 24576], P('elem', 'tm')
All inputs are finite; a program needn't handle non-finite values.
Results may differ from a plain program's by a relative error of at most 0.0003.
Values may be sent and summed in bfloat16 or wider, within the bound.
No kernel may reach another device: no remote copies, remote signals or barrier semaphores. Data moves between devices by JAX's collectives and lax.ppermute only.
A program may use at most 192 MiB of HBM per device.

v0:
```python
import jax
import jax.numpy as jnp
from jax import lax
from jax.sharding import PartitionSpec as P

loading_level = 0.1


def shifted(array, axis, by):
    size = lax.axis_size(axis)
    pairs = [(i, i + by) for i in range(size) if 0 <= i + by < size]
    return lax.ppermute(array, axis, pairs)


def entering(value, axis, join, neutral):
    count, mine = (lax.axis_size(axis), lax.axis_index(axis))
    pieces = jax.tree.map(lambda part: lax.all_gather(part, axis), value)
    so_far = jax.tree.map(
        lambda part, zero: jnp.full_like(part, 0) + jnp.asarray(zero, part.dtype), value, neutral
    )

    def hop(position, so_far):
        longer = join(so_far, jax.tree.map(lambda part: part[position], pieces))
        return jax.tree.map(lambda new, old: jnp.where(position < mine, new, old), longer, so_far)

    return lax.fori_loop(0, count - 1, hop, so_far)


def combine_estimates(earlier, later):
    return (
        earlier[0] * later[2] + later[0],
        earlier[1] * later[2] + later[1],
        earlier[2] * later[2],
    )


def weighted_gram(beam_rows, row_weight):
    return jnp.dot((beam_rows * row_weight[:, None]).T, beam_rows, precision=lax.Precision.HIGHEST)


def local(samples, taps_weight, retain):
    row_count = samples.shape[0]
    elem_width = samples.shape[1]
    tap_count = taps_weight.shape[0]
    beam_count = taps_weight.shape[2]
    sample_history = shifted(samples[row_count - (tap_count - 1) :], "tm", 1)
    extended = jnp.concatenate([sample_history, samples], 0)
    windowed = jnp.concatenate(
        [
            extended[
                tap_count - 1 - filter_tap_index : tap_count - 1 - filter_tap_index + row_count
            ]
            for filter_tap_index in range(tap_count)
        ],
        1,
    )
    filters = taps_weight.reshape(tap_count * elem_width, beam_count)
    log_retain = jnp.log(retain)
    log_total = jnp.sum(log_retain)
    row_weight = jnp.exp(log_total - jnp.cumsum(log_retain))
    factor = jnp.exp(log_total)
    mass_aggregate = jnp.sum(row_weight)
    groups = lax.axis_size("elem")
    cluster_entry = lax.axis_index("elem")
    columns = beam_count // groups
    unit_matrix = jnp.eye(beam_count, dtype=jnp.float32)
    beam_rows = lax.psum(jnp.dot(windowed, filters, preferred_element_type=jnp.float32), "elem")
    gram_block = weighted_gram(beam_rows, row_weight)
    empty = (jnp.zeros_like(gram_block), jnp.zeros((), jnp.float32), jnp.ones((), jnp.float32))
    prefix = entering((gram_block, mass_aggregate, factor), "tm", combine_estimates, empty)
    gram_sum, count_sum, unused = combine_estimates(prefix, (gram_block, mass_aggregate, factor))
    covariance_estimate = gram_sum / count_sum + loading_level * unit_matrix
    lower_factor = jnp.linalg.cholesky(covariance_estimate)
    inverse_lower = jax.scipy.linalg.solve_triangular(lower_factor, unit_matrix, lower=True)
    local_rows = lax.dynamic_slice_in_dim(inverse_lower, cluster_entry * columns, columns, 0)
    return lax.dot_general(
        local_rows, beam_rows, (((1,), (1,)), ((), ())), precision=lax.Precision.HIGHEST
    )


def solution(mesh):
    placed = (P("tm", "elem"), P(None, "elem", None), P("tm"))
    return jax.shard_map(
        local, mesh=mesh, in_specs=placed, out_specs=P("elem", "tm"), check_vma=False
    )
```

profile of v0, /device:TPU:1, one launch (start us, length us, event | category | flops | bytes accessed | tf_op | source)
XLA Modules:
  0.0 556.6 jit_solution(1617515024383423267)
XLA Ops:
  7.3 4.8 collective-permute-start
  13.1 1.1 fusion.17
  15.3 1.1 fusion.21
  19.7 1.1 fusion.29
  21.7 4.6 fusion.74
  27.4 1.3 fusion.67
  28.7 76.0 %all-reduce.6.cloned.1.call-done = f32[768,512]{1,0:T(8,128)} async-done(((f32[768,512]{1,0:T(8,128)}), f32[768,512]{1,0:T(8,128)}) %all-reduce.6.cloned.1.call-update) | async-done | bytes 1572880 | tf_op jit(solution)/shard_map/psum | solution.py:67
  104.7 5.8 %fusion.1 = f32[512,512]{1,0:T(8,128)} fusion(f32[768,512]{1,0:T(8,128)} %all-reduce.6.cloned.1.call-done, f32[768]{0:T(1024)S(1)} %get-tuple-element.205), kind=kOutput, calls=%fused_computation.4 | convolution fusion | flops 2416312320 | bytes 2624512 | tf_op jit(solution)/shard_map/dot_general | solution.py:38
  111.8 1.3 dynamic-update-slice.24
  113.8 67.2 %all-reduce.3 = (f32[32]{0:T(128)S(1)}, f32[32]{0:T(128)S(1)}) all-reduce(f32[32]{0:T(128)S(1)} %dynamic-update-slice.23, f32[32]{0:T(128)S(1)} %dynamic-update-slice.24), channel_id=1, replica_groups=mesh['elem'=8,'tm'=32] {'tm'}, use_global_device_ids=true, to_apply=%add.1 | all-reduce | flops 64 | bytes 512
  182.9 1.6 copy.16
  184.5 48.6 %all-gather.3.cloned.1.call-done = f32[16384,512]{1,0:T(8,128)} async-done(((f32[512,512]{1,0:T(8,128)}), f32[16384,512]{1,0:T(8,128)}) %all-gather.3.cloned.1.call-update) | async-done | bytes 33554448 | tf_op jit(solution)/shard_map/all_gather | solution.py:17
  233.0 161.5 %while.18 = (s32[]{:T(128)}, f32[512,512]{1,0:T(8,128)S(1)}, f32[]{:T(128)}, s32[]{:T(128)}, f32[32]{0:T(128)S(1)}, /*index=5*/f32[32,512,512]{2,1,0:T(8,128)}, f32[32]{0:T(128)S(1)}, s32[]{:T(128)}, s32[]{:T(128)}) while((s32[]{:T(128)}, f32[512,512]{1,0:T(8,128)S(1)}, f32[]{:T(128)}, s32[]{:T(128)}, f32[32]{0:T(128)S(1)}, ...), condition=%wide.region_6.7_spmd.clone, body=%wide.region_5.6_spmd.clone.sunk | while | flops 1048583 | bytes 3145910 | solution.py:26
  233.7 2.4 fusion.87
  238.9 2.4 fusion.87
  244.1 2.4 fusion.87
  249.3 2.4 fusion.87
  254.5 2.4 fusion.87
  259.7 2.4 fusion.87
  264.9 2.4 fusion.87
  270.0 2.4 fusion.87
  275.2 2.4 fusion.87
  280.4 2.4 fusion.87
  285.6 2.4 fusion.87
  290.8 2.4 fusion.87
  296.0 2.4 fusion.87
  301.2 2.4 fusion.87
  306.4 2.4 fusion.87
  311.6 2.4 fusion.87
  316.8 2.4 fusion.87
  322.0 2.4 fusion.87
  327.2 2.4 fusion.87
  332.4 2.4 fusion.87
  337.6 2.4 fusion.87
  342.8 2.4 fusion.87
  348.0 2.4 fusion.87
  353.2 2.4 fusion.87
  358.3 2.4 fusion.87
  363.5 2.4 fusion.87
  368.7 2.4 fusion.87
  373.9 2.4 fusion.87
  379.1 2.4 fusion.87
  384.3 2.4 fusion.87
  389.5 2.4 fusion.87
  396.3 11.7 %cholesky.103 = f32[128,128]{1,0:T(8,128)S(1)} custom-call(f32[128,128]{1,0:T(8,128)S(1)} %cholesky.263), custom_call_target="Cholesky" | custom-call | tf_op jit(solution)/shard_map/jit(cholesky)/cholesky | solution.py:73
  408.1 9.8 %custom-call.31 = f32[1,128,128]{1,2,0:T(8,128)S(1)} custom-call(f32[1,128,128]{2,1,0:T(8,128)S(1)} %get-tuple-element.203), custom_call_target="InvertDiagBlocksLowerTriangular" | custom-call | tf_op jit(solution)/shard_map/jit(cholesky)/cholesky | solution.py:73
  418.5 11.7 %cholesky.215 = f32[128,128]{1,0:T(8,128)S(1)} custom-call(f32[128,128]{1,0:T(8,128)S(1)} %cholesky.267), custom_call_target="Cholesky" | custom-call | tf_op jit(solution)/shard_map/jit(cholesky)/cholesky | solution.py:73
  430.6 10.0 %custom-call.32 = f32[1,128,128]{1,2,0:T(8,128)S(1)} custom-call(f32[1,128,128]{2,1,0:T(8,128)S(1)} %get-tuple-element.201), custom_call_target="InvertDiagBlocksLowerTriangular" | custom-call | tf_op jit(solution)/shard_map/jit(cholesky)/cholesky | solution.py:73
  441.1 1.6 convolution_subtract_fusion.4
  442.7 11.7 %cholesky.236 = f32[128,128]{1,0:T(8,128)S(1)} custom-call(f32[128,128]{1,0:T(8,128)S(1)} %cholesky.272), custom_call_target="Cholesky" | custom-call | tf_op jit(solution)/shard_map/jit(cholesky)/cholesky | solution.py:73
  454.6 9.8 %custom-call.33 = f32[1,128,128]{1,2,0:T(8,128)S(1)} custom-call(f32[1,128,128]{2,1,0:T(8,128)S(1)} %get-tuple-element.199), custom_call_target="InvertDiagBlocksLowerTriangular" | custom-call | tf_op jit(solution)/shard_map/jit(cholesky)/cholesky | solution.py:73
  464.7 1.3 convolution_subtract_fusion.5
  466.0 11.9 %cholesky.253 = f32[128,128]{1,0:T(8,128)S(1)} custom-call(f32[128,128]{1,0:T(8,128)S(1)} %convolution_subtract_fusion.5), custom_call_target="Cholesky" | custom-call | tf_op jit(solution)/shard_map/jit(cholesky)/cholesky | solution.py:73
  482.7 1.1 select_select_fusion
  483.8 14.9 %while.17 = (s32[]{:T(128)}, f32[512,512]{0,1:T(8,128)}, s32[4,2]{0,1:T(2,128)S(1)}, f32[4,128,128]{2,1,0:T(8,128)}, s32[]{:T(128)}) while((s32[]{:T(128)}, f32[512,512]{0,1:T(8,128)}, s32[4,2]{0,1:T(2,128)S(1)}, f32[4,128,128]{2,1,0:T(8,128)}, s32[]{:T(128)}) %tuple.57), condition=%wide.while_cond, body=%wide.while_body.sunk | while | flops 2 | bytes 393829 | solution.py:74
  484.5 2.3 dynamic-slice.9
  488.2 2.3 dynamic-slice.9
  492.0 2.3 dynamic-slice.9
  495.7 2.3 dynamic-slice.9
  498.7 40.1 %custom-call.34 = f32[4,128,128]{1,2,0:T(8,128)S(1)} custom-call(f32[4,128,128]{2,1,0:T(8,128)} %get-tuple-element.139), custom_call_target="InvertDiagBlocksLowerTriangular" | custom-call | tf_op jit(solution)/shard_map/jit(_solve_triangular)/triangular_solve | solution.py:74
  539.9 1.6 convolution_subtract_fusion.1
  541.9 2.0 convolution_subtract_fusion
  544.4 2.5 convolution_subtract_fusion.2
  547.3 2.2 fusion.53
  (156 shorter events, 65.7 us)
Async XLA Ops:
  6.5 14.3 %copy-start = (bf16[768,256]{1,0:T(8,128)(2,1)S(1)}, bf16[768,256]{1,0:T(8,128)(2,1)}, u32[]{:S(2)}) copy-start(bf16[768,256]{1,0:T(8,128)(2,1)} %param.5) | copy-start | bytes 1179652
  6.5 98.2 %all-reduce.6.cloned.1.call-start = ((), (), s32[]{:S(2)}) async-start(), calls=%async_computation | async-start | bytes 3145728 | tf_op jit(solution)/shard_map/psum | solution.py:67
  7.3 14.3 %copy-start.4 = (bf16[16,256,512]{2,1,0:T(8,128)(2,1)S(1)}, bf16[16,256,512]{2,1,0:T(8,128)(2,1)}, u32[]{:S(2)}) copy-start(bf16[16,256,512]{2,1,0:T(8,128)(2,1)} %param.6) | copy-start | bytes 12582916
  7.3 5.8 %collective-permute-start = (bf16[15,256]{1,0:T(8,128)(2,1)S(1)}, bf16[15,256]{1,0:T(8,128)(2,1)S(1)}, u32[]{:S(2)}, u32[]{:S(2)}) collective-permute-start(bf16[15,256]{1,0:T(8,128)(2,1)S(1)} %slice.169), channel_id=1, source_target_pairs={{0,1},{1,2},{2,3},{3,4},{4,5},{5,6},{6,7},{7,8},{8,9},{9,10},{10,1... | collective-permute-start | bytes 23048 | tf_op jit(solution)/shard_map/ppermute | solution.py:12
  21.6 4.7 copy-start.3
  26.2 85.0 %copy-start.5 = (u32[256]{0:T(256)S(1)}, u32[256]{0:T(256)}, u32[]{:S(2)}) copy-start(u32[256]{0:T(256)} %constant.208) | copy-start | bytes 3076
  26.2 206.8 %all-gather.3.cloned.1.call-start = ((), (), s32[]{:S(2)}) async-start(), calls=%async_computation.1 | async-start | bytes 34603008 | tf_op jit(solution)/shard_map/all_gather | solution.py:17
  396.3 34.3 %copy-start.2 = (f32[512,512]{1,0:T(8,128)}, f32[512,512]{1,0:T(8,128)S(1)}, u32[]{:S(2)}) copy-start(f32[512,512]{1,0:T(8,128)S(1)} %fusion.3) | copy-start | bytes 3145732
  440.7 106.6 %copy-start.1 = (f32[768,512]{1,0:T(8,128)S(1)}, f32[768,512]{1,0:T(8,128)}, u32[]{:S(2)}) copy-start(f32[768,512]{1,0:T(8,128)} %all-reduce.6.cloned.1.call-done) | copy-start | bytes 4718596
Sparse Core Ops, SparseCore 0:
  26.4 78.2 all-reduce.5
  110.6 122.3 all-gather.2
where the time goes:
time: 566 us; the launch traced here: 557 us
  other arithmetic  209 us (37%)
  waiting for transfers between devices  125 us (22%)
  blocking collectives  67.2 us (12%)
  local copies, waits for them, and re-layouts  63.6 us (11%)
  loops' own time  44.4 us (8%)
  matrix products  25.2 us (4%)
  between operations  18 us (3%)
    another operation x14, other arithmetic, local(): lower_factor = jnp.linalg.cholesky(covariance_estimate)  78.8 us
    psum x1, waiting for transfers between devices, local(): lax.psum(jnp.dot(windowed, filters, preferred_element_type=jnp.float32),...  76 us
    select_n x31, other arithmetic, hop(): jnp.where(position < mine, new, old)  75.8 us
    unnamed x1, blocking collectives  67.2 us
    all_gather x1, waiting for transfers between devices, entering(): pieces = jax.tree.map(lambda part: lax.all_gather(part, axis), value)  48.6 us
    another operation x1, loops' own time, entering(): return lax.fori_loop(0, count - 1, hop, so_far)  44.4 us
    dynamic_slice x62, local copies, waits for them, and re-layouts, hop(): longer = join(so_far, jax.tree.map(lambda part: part[position], pieces))  41.3 us
    another operation x3, other arithmetic, local(): jax.scipy.linalg.solve_triangular(lower_factor, unit_matrix, lower=True)  41.2 us
  transfers between devices with their start and end apart: 3, of which 2 were waited for; matrix products, arithmetic and copies ran while one was open for 2% of the time, Pallas kernels for 0%

commit v1 on v0

--- a/solution.py
+++ b/solution.py
@@ -64,7 +64,10 @@
     cluster_entry = lax.axis_index("elem")
     columns = beam_count // groups
     unit_matrix = jnp.eye(beam_count, dtype=jnp.float32)
-    beam_rows = lax.psum(jnp.dot(windowed, filters, preferred_element_type=jnp.float32), "elem")
+    beam_rows = jnp.sum(
+        lax.all_gather(jnp.dot(windowed, filters, preferred_element_type=jnp.float32), "elem"),
+        axis=0,
+    )
     gram_block = weighted_gram(beam_rows, row_weight)
     empty = (jnp.zeros_like(gram_block), jnp.zeros((), jnp.float32), jnp.ones((), jnp.float32))
     prefix = entering((gram_block, mass_aggregate, factor), "tm", combine_estimates, empty)

time: 566 us -> 617 us (1.090)
  waiting for transfers between devices: 125 us -> 182 us
  loops' own time: 44.4 us -> 37.1 us
    all_gather x0 -> x1, waiting for transfers between devices: none -> 134 us  [local(): lax.all_gather(jnp.dot(windowed, filters, preferred_element_type=jnp.floa...]
    psum x1 -> x0, waiting for transfers between devices: 76 us -> none  [local(): lax.psum(jnp.dot(windowed, filters, preferred_element_type=jnp.float32),...]
    another operation x1, loops' own time: 44.4 us -> 37.1 us  [entering(): return lax.fori_loop(0, count - 1, hop, so_far)]
    reduce_sum x0 -> x1, other arithmetic: none -> 6.32 us  [local(): jnp.sum(lax.all_gather(jnp.dot(windowed, filters, preferred_element_type=...]
where the time goes in v1:
time: 617 us; the launch traced here: 606 us
  other arithmetic  214 us (35%)
  waiting for transfers between devices  182 us (29%)
  blocking collectives  63.7 us (10%)
  local copies, waits for them, and re-layouts  62.9 us (10%)
  loops' own time  37.1 us (6%)
  matrix products  24.3 us (4%)
  between operations  17.9 us (3%)
    all_gather x1, waiting for transfers between devices, local(): lax.all_gather(jnp.dot(windowed, filters, preferred_element_type=jnp.floa...  134 us
    another operation x14, other arithmetic, local(): lower_factor = jnp.linalg.cholesky(covariance_estimate)  78.7 us
    select_n x31, other arithmetic, hop(): jnp.where(position < mine, new, old)  72.2 us
    unnamed x1, blocking collectives  63.7 us
    all_gather x1, waiting for transfers between devices, entering(): pieces = jax.tree.map(lambda part: lax.all_gather(part, axis), value)  47.4 us
    another operation x3, other arithmetic, local(): jax.scipy.linalg.solve_triangular(lower_factor, unit_matrix, lower=True)  41.2 us
    another operation x1, loops' own time, entering(): return lax.fori_loop(0, count - 1, hop, so_far)  37.1 us
    dynamic_slice x62, local copies, waits for them, and re-layouts, hop(): longer = join(so_far, jax.tree.map(lambda part: part[position], pieces))  36.8 us
  transfers between devices with their start and end apart: 3, of which 2 were waited for; matrix products, arithmetic and copies ran while one was open for 2% of the time, Pallas kernels for 0%

profile of v1, /device:TPU:1, one launch (start us, length us, event | category | flops | bytes accessed | tf_op | source)
XLA Modules:
  0.0 605.9 jit_solution(7416201626087092520)
XLA Ops:
  7.3 4.8 collective-permute-start
  21.7 4.6 fusion.74
  27.5 1.4 fusion.67
  28.8 134.2 %all-gather.5.cloned.1.call-done = f32[6144,512]{1,0:T(8,128)} async-done(((f32[768,512]{1,0:T(8,128)}), f32[6144,512]{1,0:T(8,128)}) %all-gather.5.cloned.1.call-update) | async-done | bytes 12582928 | tf_op jit(solution)/shard_map/all_gather | solution.py:68
  163.1 6.3 %reduce_sum.28 = f32[768,512]{1,0:T(8,128)S(1)} reduce(f32[8,768,512]{2,1,0:T(8,128)} %bitcast.72, f32[]{:T(128)} %copy.76), dimensions={0}, to_apply=%region_0.0 | reduce | flops 2752512 | bytes 14155780 | tf_op jit(solution)/shard_map/reduce_sum | solution.py:67
  169.4 3.9 fusion.1
  174.7 1.4 dynamic-update-slice.24
  176.9 63.7 %all-reduce.3 = (f32[32]{0:T(128)S(1)}, f32[32]{0:T(128)S(1)}) all-reduce(f32[32]{0:T(128)S(1)} %dynamic-update-slice.23, f32[32]{0:T(128)S(1)} %dynamic-update-slice.24), channel_id=1, replica_groups=mesh['elem'=8,'tm'=32] {'tm'}, use_global_device_ids=true, to_apply=%add.1 | all-reduce | flops 64 | bytes 512
  241.7 2.6 copy.16
  244.3 47.4 %all-gather.7.cloned.1.call-done = f32[16384,512]{1,0:T(8,128)} async-done(((f32[512,512]{1,0:T(8,128)}), f32[16384,512]{1,0:T(8,128)}) %all-gather.7.cloned.1.call-update) | async-done | bytes 33554448 | tf_op jit(solution)/shard_map/all_gather | solution.py:17
  291.7 146.0 %while.18 = (s32[]{:T(128)}, f32[512,512]{1,0:T(8,128)S(1)}, f32[]{:T(128)}, s32[]{:T(128)}, f32[32]{0:T(128)S(1)}, /*index=5*/f32[32,512,512]{2,1,0:T(8,128)}, f32[32]{0:T(128)S(1)}, s32[]{:T(128)}, s32[]{:T(128)}) while((s32[]{:T(128)}, f32[512,512]{1,0:T(8,128)S(1)}, f32[]{:T(128)}, s32[]{:T(128)}, f32[32]{0:T(128)S(1)}, ...), condition=%wide.region_6.7_spmd.clone, body=%wide.region_5.6_spmd.clone.sunk | while | flops 1048583 | bytes 3145910 | solution.py:26
  292.2 2.3 fusion.87
  296.9 2.3 fusion.87
  301.6 2.3 fusion.87
  306.3 2.3 fusion.87
  311.0 2.3 fusion.87
  315.7 2.3 fusion.87
  320.4 2.3 fusion.87
  325.1 2.3 fusion.87
  329.8 2.3 fusion.87
  334.5 2.3 fusion.87
  339.2 2.3 fusion.87
  343.9 2.3 fusion.87
  348.6 2.3 fusion.87
  353.3 2.3 fusion.87
  358.0 2.3 fusion.87
  362.7 2.3 fusion.87
  367.4 2.3 fusion.87
  372.1 2.3 fusion.87
  376.8 2.3 fusion.87
  381.5 2.3 fusion.87
  386.2 2.3 fusion.87
  390.9 2.3 fusion.87
  395.6 2.3 fusion.87
  400.3 2.3 fusion.87
  405.0 2.3 fusion.87
  409.7 2.3 fusion.87
  414.4 2.3 fusion.87
  419.1 2.3 fusion.87
  423.8 2.3 fusion.87
  428.4 2.3 fusion.87
  433.1 2.3 fusion.87
  439.7 1.8 select_add_fusion
  441.4 1.3 copy.17
  442.8 1.4 fusion.3
  445.2 11.7 %cholesky.103 = f32[128,128]{1,0:T(8,128)S(1)} custom-call(f32[128,128]{1,0:T(8,128)S(1)} %cholesky.263), custom_call_target="Cholesky" | custom-call | tf_op jit(solution)/shard_map/jit(cholesky)/cholesky | solution.py:76
  457.0 9.8 %custom-call.31 = f32[1,128,128]{1,2,0:T(8,128)S(1)} custom-call(f32[1,128,128]{2,1,0:T(8,128)S(1)} %get-tuple-element.203), custom_call_target="InvertDiagBlocksLowerTriangular" | custom-call | tf_op jit(solution)/shard_map/jit(cholesky)/cholesky | solution.py:76
  469.3 11.7 %cholesky.215 = f32[128,128]{1,0:T(8,128)S(1)} custom-call(f32[128,128]{1,0:T(8,128)S(1)} %cholesky.267), custom_call_target="Cholesky" | custom-call | tf_op jit(solution)/shard_map/jit(cholesky)/cholesky | solution.py:76
  481.4 10.0 %custom-call.32 = f32[1,128,128]{1,2,0:T(8,128)S(1)} custom-call(f32[1,128,128]{2,1,0:T(8,128)S(1)} %get-tuple-element.201), custom_call_target="InvertDiagBlocksLowerTriangular" | custom-call | tf_op jit(solution)/shard_map/jit(cholesky)/cholesky | solution.py:76
  491.8 1.5 convolution_subtract_fusion.4
  493.4 11.7 %cholesky.236 = f32[128,128]{1,0:T(8,128)S(1)} custom-call(f32[128,128]{1,0:T(8,128)S(1)} %cholesky.272), custom_call_target="Cholesky" | custom-call | tf_op jit(solution)/shard_map/jit(cholesky)/cholesky | solution.py:76
  505.2 9.8 %custom-call.33 = f32[1,128,128]{1,2,0:T(8,128)S(1)} custom-call(f32[1,128,128]{2,1,0:T(8,128)S(1)} %get-tuple-element.199), custom_call_target="InvertDiagBlocksLowerTriangular" | custom-call | tf_op jit(solution)/shard_map/jit(cholesky)/cholesky | solution.py:76
  515.3 1.3 convolution_subtract_fusion.5
  516.7 11.9 %cholesky.253 = f32[128,128]{1,0:T(8,128)S(1)} custom-call(f32[128,128]{1,0:T(8,128)S(1)} %convolution_subtract_fusion.5), custom_call_target="Cholesky" | custom-call | tf_op jit(solution)/shard_map/jit(cholesky)/cholesky | solution.py:76
  534.3 14.4 %while.17 = (s32[]{:T(128)}, f32[512,512]{0,1:T(8,128)}, s32[4,2]{0,1:T(2,128)S(1)}, f32[4,128,128]{2,1,0:T(8,128)}, s32[]{:T(128)}) while((s32[]{:T(128)}, f32[512,512]{0,1:T(8,128)}, s32[4,2]{0,1:T(2,128)S(1)}, f32[4,128,128]{2,1,0:T(8,128)}, s32[]{:T(128)}) %tuple.57), condition=%wide.while_cond, body=%wide.while_body.sunk | while | flops 2 | bytes 393829 | solution.py:77
  534.9 2.3 dynamic-slice.9
  538.5 2.3 dynamic-slice.9
  542.1 2.3 dynamic-slice.9
  545.8 2.2 dynamic-slice.9
  548.7 40.1 %custom-call.34 = f32[4,128,128]{1,2,0:T(8,128)S(1)} custom-call(f32[4,128,128]{2,1,0:T(8,128)} %get-tuple-element.139), custom_call_target="InvertDiagBlocksLowerTriangular" | custom-call | tf_op jit(solution)/shard_map/jit(_solve_triangular)/triangular_solve | solution.py:77
  589.2 1.6 convolution_subtract_fusion.1
  591.2 2.0 convolution_subtract_fusion
  593.6 2.5 convolution_subtract_fusion.2
  596.6 2.2 fusion.53
  (155 shorter events, 67.0 us)
Async XLA Ops:
  6.5 14.3 %copy-start = (bf16[768,256]{1,0:T(8,128)(2,1)S(1)}, bf16[768,256]{1,0:T(8,128)(2,1)}, u32[]{:S(2)}) copy-start(bf16[768,256]{1,0:T(8,128)(2,1)} %param.5) | copy-start | bytes 1179652
  6.5 156.5 %all-gather.5.cloned.1.call-start = ((), (), s32[]{:S(2)}) async-start(), calls=%async_computation | async-start | bytes 14155776 | tf_op jit(solution)/shard_map/all_gather | solution.py:68
  7.3 14.3 %copy-start.3 = (bf16[16,256,512]{2,1,0:T(8,128)(2,1)S(1)}, bf16[16,256,512]{2,1,0:T(8,128)(2,1)}, u32[]{:S(2)}) copy-start(bf16[16,256,512]{2,1,0:T(8,128)(2,1)} %param.6) | copy-start | bytes 12582916
  7.3 5.8 collective-permute-start
  21.6 4.7 copy-start.2
  26.3 265.4 %all-gather.7.cloned.1.call-start = ((), (), s32[]{:S(2)}) async-start(), calls=%async_computation.1 | async-start | bytes 34603008 | tf_op jit(solution)/shard_map/all_gather | solution.py:17
  163.1 11.0 %copy-start.4 = (u32[256]{0:T(256)S(1)}, u32[256]{0:T(256)}, u32[]{:S(2)}) copy-start(u32[256]{0:T(256)} %constant.208) | copy-start | bytes 3076
  444.2 1.0 copy-start.1
Sparse Core Ops, SparseCore 0:
  26.4 136.6 all-gather.4
  173.4 118.1 all-gather.6
